TPU v7x, 256 devices: a whole 4x4x8 slice. The times are simulated.
256 devices in a mesh: req: 32 (over z, x), tp: 8 (over y, core).
Axes of the slice: x: 4, y: 4, z: 8, core: 2. Of those that a mesh axis runs over, the one named last changes fastest.
Arguments:
- hidden_in: bfloat16 [192, 64, 3072], P('req', None, 'tp'), may hold values from -3 to 3
- request_order: int32 [192], replicated, may hold values from 0 to 191, as said below
- norm_gain: bfloat16 [3072], replicated, may hold values from 0.099609375 to 1.8984375
- w_query: bfloat16 [3072, 3072], P(None, 'tp'), may hold values from -0.109375 to 0.109375
- key_weight: bfloat16 [3072, 1024], P(None, 'tp'), may hold values from -0.4375 to 0.4375
- value_weight: bfloat16 [3072, 1024], P(None, 'tp'), may hold values from -0.109375 to 0.109375
- w_out: bfloat16 [3072, 3072], P('tp'), may hold values from -0.109375 to 0.109375
- key_cache: bfloat16 [192, 8, 3456, 128], P('req', 'tp'), may hold values from -360 to 360
- cached_values: bfloat16 [192, 8, 3456, 128], P('req', 'tp'), may hold values from -24 to 24
- cache_lengths: int32 [192], P('req'), may hold values from 864 to 3456, as said below
- tree_parent: int32 [192, 64], P('req'), may hold values from 0 to 63, as said below
- kept_nodes: int32 [192, 8], P('req'), may hold values from 0 to 63
Outputs:
- layer_out: bfloat16 [192, 64, 3072], P('req', None, 'tp')
- appended: bfloat16 [192, 2, 8, 8, 128], P('req', None, None, 'tp')
Inputs may be any that keep to these rules, and one draw needn't show every extreme that they name: `request_order`: each request is held by exactly one slot. The 6 requests of one device's rows go to 6 different devices of req, and the slots of one device hold requests of 6 different devices. `cache_lengths`: some slot has exactly 3456 live positions. `tree_parent`: node 0 has parent 0; every other node's parent has a lower index.
All inputs are finite; a program needn't handle non-finite values.
Results may differ from a plain program's by a relative error of at most 0.0085.
The roundings to bfloat16 on the way count: a program that leaves them out, or rounds other values in their place, can miss the bound.
Values may be sent and summed in bfloat16 or wider, within the bound.
A program may use at most 128 MiB of HBM per device.

v0:
```python
import jax
import jax.numpy as jnp
from jax import lax
from jax.sharding import PartitionSpec as P

HEAD_WIDTH = 128
NORM_EPSILON = 1e-05


def rotary_embedding(vectors, token_positions):
    half_dim = vectors.shape[-1] // 2
    frequency = 500000.0 ** (-jnp.arange(half_dim, dtype=jnp.float32) * 2.0 / vectors.shape[-1])
    angles = token_positions[..., None] * frequency
    cosine = jnp.cos(angles)[..., None, :]
    sine = jnp.sin(angles)[..., None, :]
    first_half = vectors[..., :half_dim]
    second_half = vectors[..., half_dim:]
    return jnp.concatenate(
        [first_half * cosine - second_half * sine, second_half * cosine + first_half * sine],
        axis=-1,
    )


def body(
    hidden_in,
    request_order,
    norm_gain,
    w_query,
    key_weight,
    value_weight,
    w_out,
    key_cache,
    cached_values,
    cache_lengths,
    tree_parent,
    kept_nodes,
):
    slots_here = key_cache.shape[0]
    tree_length = hidden_in.shape[1]
    width_local = hidden_in.shape[2]
    local_groups = key_cache.shape[1]
    local_heads = w_query.shape[1] // HEAD_WIDTH
    group_width = local_heads // local_groups
    slot_ids = lax.axis_index("req") * slots_here + jnp.arange(slots_here, dtype=jnp.int32)
    own_order = request_order[slot_ids]
    piece = lax.all_gather(hidden_in, "req", axis=0, tiled=True)
    piece_ids = jnp.arange(piece.shape[0], dtype=jnp.int32)
    chooser = (own_order[:, None] == piece_ids[None, :]).astype(jnp.bfloat16)
    dealt = jnp.einsum("rm,mtd->rtd", chooser, piece, preferred_element_type=jnp.float32).astype(
        jnp.bfloat16
    )
    widened = lax.all_gather(dealt, "tp", axis=2, tiled=True).astype(jnp.float32)
    normalized_input = (
        widened
        * lax.rsqrt(jnp.mean(widened * widened, axis=-1, keepdims=True) + NORM_EPSILON)
        * norm_gain.astype(jnp.float32)
    ).astype(jnp.bfloat16)
    flat_rows = normalized_input.reshape(slots_here * tree_length, normalized_input.shape[2])
    query_rows = jnp.dot(flat_rows, w_query, preferred_element_type=jnp.float32).reshape(
        slots_here, tree_length, local_heads, HEAD_WIDTH
    )
    fresh_keys = jnp.dot(flat_rows, key_weight, preferred_element_type=jnp.float32).reshape(
        slots_here, tree_length, local_groups, HEAD_WIDTH
    )
    fresh_values = (
        jnp.dot(flat_rows, value_weight, preferred_element_type=jnp.float32)
        .astype(jnp.bfloat16)
        .reshape(slots_here, tree_length, local_groups, HEAD_WIDTH)
    )
    node_ids = jnp.arange(tree_length, dtype=jnp.int32)
    parent_link = (
        (tree_parent[:, :, None] == node_ids[None, None, :]) & (node_ids[None, :, None] > 0)
    ).astype(jnp.float32)
    ancestry = jnp.eye(tree_length, dtype=jnp.float32)[None] + parent_link
    for sweep in range(tree_length.bit_length()):
        ancestry = jnp.minimum(
            jnp.einsum("rij,rjk->rik", ancestry, ancestry, precision=lax.Precision.HIGHEST), 1.0
        )
    token_positions = cache_lengths.astype(jnp.float32)[:, None] + jnp.sum(ancestry, axis=-1) - 1.0
    rotated_query = (
        rotary_embedding(query_rows, token_positions)
        .astype(jnp.bfloat16)
        .reshape(slots_here, tree_length, local_groups, group_width, HEAD_WIDTH)
    )
    key_rot = rotary_embedding(fresh_keys, token_positions).astype(jnp.bfloat16)
    score_scale = HEAD_WIDTH ** (-0.5)
    cache_scores = (
        jnp.einsum(
            "rtgqd,rgcd->rgqtc", rotated_query, key_cache, preferred_element_type=jnp.float32
        )
        * score_scale
    )
    live_keys = jnp.arange(key_cache.shape[2], dtype=jnp.int32)[None, :] < cache_lengths[:, None]
    cache_scores = jnp.where(live_keys[:, None, None, None, :], cache_scores, -jnp.inf)
    tree_scores = (
        jnp.einsum("rtgqd,rsgd->rgqts", rotated_query, key_rot, preferred_element_type=jnp.float32)
        * score_scale
    )
    tree_scores = jnp.where(ancestry[:, None, None] > 0, tree_scores, -jnp.inf)
    row_max = jnp.maximum(jnp.max(cache_scores, axis=-1), jnp.max(tree_scores, axis=-1))
    cache_exp = jnp.exp(cache_scores - row_max[..., None])
    tree_exp = jnp.exp(tree_scores - row_max[..., None])
    row_total = jnp.sum(cache_exp, axis=-1) + jnp.sum(tree_exp, axis=-1)
    cache_weights = (cache_exp / row_total[..., None]).astype(jnp.bfloat16)
    tree_weights = (tree_exp / row_total[..., None]).astype(jnp.bfloat16)
    attended = jnp.einsum(
        "rgqtc,rgcd->rtgqd", cache_weights, cached_values, preferred_element_type=jnp.float32
    )
    attended = attended + jnp.einsum(
        "rgqts,rsgd->rtgqd", tree_weights, fresh_values, preferred_element_type=jnp.float32
    )
    attended = attended.astype(jnp.bfloat16).reshape(
        slots_here, tree_length, local_heads * HEAD_WIDTH
    )
    keep_select = (kept_nodes[:, :, None] == node_ids[None, None, :]).astype(jnp.bfloat16)
    stacked = jnp.stack([key_rot, fresh_values], axis=1)
    appended = jnp.einsum(
        "rkt,rxtgd->rxkgd", keep_select, stacked, preferred_element_type=jnp.float32
    ).astype(jnp.bfloat16)
    partials = jnp.dot(
        attended.reshape(-1, attended.shape[2]), w_out, preferred_element_type=jnp.float32
    )
    summed = lax.psum(partials, "tp")
    my_share = lax.dynamic_slice_in_dim(summed, lax.axis_index("tp") * width_local, width_local, 1)
    layer_out = (my_share.reshape(dealt.shape) + dealt.astype(jnp.float32)).astype(jnp.bfloat16)
    return (layer_out, appended)


def solution(mesh):
    placed = (
        P("req", None, "tp"),
        P(),
        P(),
        P(None, "tp"),
        P(None, "tp"),
        P(None, "tp"),
        P("tp", None),
        P("req", "tp", None, None),
        P("req", "tp", None, None),
        P("req"),
        P("req", None),
        P("req", None),
    )
    return jax.shard_map(
        body,
        mesh=mesh,
        in_specs=placed,
        out_specs=(P("req", None, "tp"), P("req", None, None, "tp", None)),
        check_vma=False,
    )
```

profile of v0, /device:TPU:2, one launch (start us, length us, event | category | flops | bytes accessed | tf_op | source)
XLA Modules:
  0.0 284.8 jit_solution(10960639715566622475)
XLA Ops:
  7.2 0.0 copy-start
  7.2 0.0 all-gather.3.cloned.1.call-start
  7.2 0.7 all-gather.3.cloned.1.call-update
  7.9 0.0 all-gather.5.cloned.1.call-start
  8.0 1.3 gather_fusion
  9.3 0.0 copy-start.3
  9.3 0.0 copy-start.5
  9.3 106.1 %all-gather.3.cloned.1.call-done = bf16[192,64,384]{2,1,0:T(8,128)(2,1)} async-done(((bf16[6,64,384]{2,1,0:T(8,128)(2,1)}), bf16[192,64,384]{2,1,0:T(8,128)(2,1)}) %all-gather.3.cloned.1.call-update) | async-done | bytes 9437200 | tf_op jit(solution)/shard_map/all_gather | solution.py:46
  115.4 11.9 %fusion.3 = bf16[6,64,384]{2,0,1:T(8,128)(2,1)S(1)} fusion(bf16[192,64,384]{2,1,0:T(8,128)(2,1)} %all-gather.3.cloned.1.call-done, s32[6]{0:T(128)S(1)} %gather_fusion), kind=kOutput, calls=%fused_computation.7 | convolution fusion | flops 56624256 | bytes 9732120 | tf_op jit(solution)/shard_map/rm,mtd->rtd/dot_general | solution.py:49
  127.3 0.8 copy.78
  128.1 0.0 all-gather.5.cloned.1.call-update
  128.1 0.0 all-reduce.2.cloned.1.call-start
  128.3 0.5 convolution_minimum_fusion.6
  128.7 0.3 convolution_minimum_fusion.5
  129.0 0.3 convolution_minimum_fusion.4
  129.4 0.3 convolution_minimum_fusion.3
  129.7 0.3 convolution_minimum_fusion.2
  130.0 0.3 convolution_minimum_fusion.1
  130.4 0.4 fusion.63
  130.8 0.1 copy.54
  131.0 4.5 %copy.51 = bf16[3072,384]{0,1:T(8,128)(2,1)} copy(bf16[3072,384]{1,0:T(8,128)(2,1)} %param.15) | data formatting | bytes 4718592 | tf_op args[3]
  135.5 0.1 add_add_fusion
  135.5 0.8 multiply_cosine_fusion.1
  136.3 0.1 iota_compare_fusion.1
  136.4 19.0 %all-gather.5.cloned.1.call-done = bf16[6,64,3072]{2,1,0:T(8,128)(2,1)} async-done(((bf16[6,64,384]{2,1,0:T(8,128)(2,1)}), bf16[6,64,3072]{2,1,0:T(8,128)(2,1)}) %all-gather.5.cloned.1.call-update) | async-done | bytes 2359312 | tf_op jit(solution)/shard_map/all_gather | solution.py:52
  155.4 2.4 fusion.11
  157.7 2.4 fusion.13
  160.2 0.0 slice-start
  160.2 0.8 convolution_bitcast_fusion
  161.0 0.8 fusion.38
  161.8 0.0 slice-start.1
  161.8 1.4 fusion.14
  163.2 0.3 subtract_convert_fusion
  163.6 6.9 %fusion.2 = (f32[6,3,64]{2,1,0:T(4,128)S(1)}, f32[6,64,3,3456]{3,1,2,0:T(8,128)}) fusion(pred[6,3456]{1,0:T(8,128)(4,1)S(1)} %iota_compare_fusion.1, bf16[6,1,3456,128]{3,2,1,0:T(8,128)(2,1)S(1)} %bitcast.146, bf16[6,64,3,64]{3,1,2,0:T(8,128)(2,1)S(1)} %get-tuple-element.11, bf16[6,64,3,64]{3,1,2,0:T(8,128)(2,1)S(1)} %get-tuple-element.10), kind=kOutput, calls=%fused_computation.6 | convolution fusion | flops 1031748480 | bytes 21553920 | tf_op jit(solution)/shard_map/rtgqd,rgcd->rgqtc/dot_general | solution.py:88
  170.5 0.4 fusion.64
  171.0 0.1 fusion.27
  171.1 9.2 %fusion.1 = f32[6,3,64]{2,1,0:T(4,128)S(1)} fusion(f32[6,64,3,3456]{3,1,2,0:T(8,128)} %get-tuple-element.19, f32[6,3,64]{2,1,0:T(4,128)S(1)} %max.9, pred[6,3456]{1,0:T(8,128)(4,1)S(1)} %iota_compare_fusion.1), kind=kLoop, calls=%fused_computation.5 | loop fusion | flops 15924096 | bytes 15955200 | tf_op jit(solution)/shard_map/reduce_sum | solution.py:103
  180.3 1.9 convolution_convert_fusion
  182.2 10.3 %fusion.17 = f32[6,128,3,64]{1,3,2,0:T(8,128)S(1)} fusion(bf16[6,1,3456,128]{3,2,1,0:T(8,128)(2,1)} %param.20, f32[6,3,64]{2,1,0:T(4,128)S(1)} %add.98, f32[6,3,64]{2,1,0:T(4,128)S(1)} %max.9, f32[6,64,3,3456]{3,1,2,0:T(8,128)} %get-tuple-element.19, pred[6,3456]{1,0:T(8,128)(4,1)S(1)} %iota_compare_fusion.1), kind=kOutput, calls=%fused_computation.25 | convolution fusion | flops 1039122432 | bytes 21853440 | tf_op jit(solution)/shard_map/rgqtc,rgcd->rtgqd/dot_general | solution.py:106
  192.5 0.3 fusion.24
  192.8 0.3 copy.56
  193.1 0.0 copy-start.6
  193.1 3.5 %fusion.28 = f32[384,3072]{1,0:T(8,128)} fusion(bf16[384,3072]{1,0:T(8,128)(2,1)S(1)} %copy-done, bf16[48,8,3,128]{3,2,1,0:T(4,128)(2,1)S(1)} %bitcast.149), kind=kOutput, calls=%fused_computation.48 | convolution fusion | flops 905969664 | bytes 7372800 | tf_op jit(solution)/shard_map/dot_general | solution.py:120
  196.7 0.0 all-reduce.2.cloned.1.call-update
  196.7 0.8 fusion.25
  197.5 78.8 %all-reduce.2.cloned.1.call-done = f32[384,3072]{1,0:T(8,128)} async-done(((f32[384,3072]{1,0:T(8,128)}), f32[384,3072]{1,0:T(8,128)}) %all-reduce.2.cloned.1.call-update) | async-done | bytes 4718608 | tf_op jit(solution)/shard_map/psum | solution.py:123
  276.3 1.1 constant_dynamic-slice_fusion
  277.4 0.8 add_convert_fusion
  (24 shorter events, 0.1 us)
Async XLA Ops:
  7.2 185.9 %copy-start = (bf16[384,3072]{1,0:T(8,128)(2,1)S(1)}, bf16[384,3072]{1,0:T(8,128)(2,1)}, u32[]{:S(2)}) copy-start(bf16[384,3072]{1,0:T(8,128)(2,1)} %param.18) | copy-start | bytes 7077892
  7.2 108.2 %all-gather.3.cloned.1.call-start = ((), (), s32[]{:S(2)}) async-start(), calls=%async_computation | async-start | bytes 9732096 | tf_op jit(solution)/shard_map/all_gather | solution.py:46
  7.9 147.5 %all-gather.5.cloned.1.call-start = ((), (), s32[]{:S(2)}) async-start(), calls=%async_computation.1 | async-start | bytes 2654208 | tf_op jit(solution)/shard_map/all_gather | solution.py:52
  9.3 118.9 %copy-start.4 = (s32[6]{0:T(128)S(1)}, s32[6]{0:T(128)}, u32[]{:S(2)}) copy-start(s32[6]{0:T(128)} %param.21) | copy-start | bytes 76
  9.3 118.9 %copy-start.3 = (bf16[3072]{0:T(1024)(128)(2,1)S(1)}, bf16[3072]{0:T(1024)(128)(2,1)}, u32[]{:S(2)}) copy-start(bf16[3072]{0:T(1024)(128)(2,1)} %param.14) | copy-start | bytes 18436
  9.3 118.9 %copy-start.5 = (s32[6,64]{1,0:T(8,128)S(1)}, s32[6,64]{1,0:T(8,128)}, u32[]{:S(2)}) copy-start(s32[6,64]{1,0:T(8,128)} %param.22) | copy-start | bytes 4612
  128.1 148.2 %all-reduce.2.cloned.1.call-start = ((), (), s32[]{:S(2)}) async-start(), calls=%async_computation.2 | async-start | bytes 9437184 | tf_op jit(solution)/shard_map/psum | solution.py:123
  155.4 4.8 %copy-start.2 = (bf16[3072,128]{1,0:T(8,128)(2,1)S(1)}, bf16[3072,128]{1,0:T(8,128)(2,1)}, u32[]{:S(2)}) copy-start(bf16[3072,128]{1,0:T(8,128)(2,1)} %param.16) | copy-start | bytes 2359300
  155.4 6.4 %copy-start.1 = (bf16[3072,384]{0,1:T(8,128)(2,1)S(1)}, bf16[3072,384]{0,1:T(8,128)(2,1)}, u32[]{:S(2)}) copy-start(bf16[3072,384]{0,1:T(8,128)(2,1)} %copy.51) | copy-start | bytes 7077892
  160.2 3.4 %slice-start = ((s8[5308416]{0:T(1024)(128)(4,1)}), s8[4194304]{0:T(1024)(128)(4,1)S(1)}, s32[]{:S(2)}) async-start(s8[5308416]{0:T(1024)(128)(4,1)} %bitcast.145), calls=%async_computation.3 | async-start | bytes 8388608
  161.8 1.7 slice-start.1
  193.1 3.6 %copy-start.6 = (s32[6,8]{1,0:T(8,128)S(1)}, s32[6,8]{1,0:T(8,128)}, u32[]{:S(2)}) copy-start(s32[6,8]{1,0:T(8,128)} %param.23) | copy-start | bytes 580
Sparse Core Ops, SparseCore 0:
  10.6 104.8 all-gather.2
  128.2 27.0 all-gather.4
  196.8 79.4 all-reduce.1
where the time goes:
time: 285 us
  waiting for transfers between devices  205 us (72%)
  matrix products  40.8 us (14%)
  other arithmetic  17 us (6%)
  between operations  14.1 us (5%)
  local copies, waits for them, and re-layouts  8.1 us (3%)
    all_gather x1, waiting for transfers between devices, body(): piece = lax.all_gather(hidden_in, 'req', axis=0, tiled=True)  106 us
    psum x1, waiting for transfers between devices, body(): summed = lax.psum(partials, 'tp')  78.8 us
    all_gather x1, waiting for transfers between devices, body(): lax.all_gather(dealt, 'tp', axis=2, tiled=True).astype(jnp.float32)  19 us
    dot_general x1, matrix products, body(): jnp.einsum('rm,mtd->rtd', chooser, piece, preferred_element_type=jnp.floa...  11.9 us
    dot_general x1, matrix products, body(): jnp.einsum('rgqtc,rgcd->rtgqd', cache_weights, cached_values, preferred_e...  10.3 us
    reduce_sum x2, other arithmetic, body(): row_total = jnp.sum(cache_exp, axis=-1) + jnp.sum(tree_exp, axis=-1)  9.32 us
    dot_general x1, matrix products, body(): jnp.einsum('rtgqd,rgcd->rgqtc', rotated_query, key_cache, preferred_eleme...  6.91 us
  transfers between devices with their start and end apart: 3, of which 3 were waited for; matrix products, arithmetic and copies ran while one was open for 4% of the time, Pallas kernels for 0%

commit v1 on v0

--- a/solution.py
+++ b/solution.py
@@ -5,6 +5,28 @@
 
 HEAD_WIDTH = 128
 NORM_EPSILON = 1e-05
+
+
+def laid_out(parts, dim):
+    dims = list(parts.shape[1:])
+    dims[dim] *= parts.shape[0]
+    return jnp.moveaxis(parts, 0, dim).reshape(dims)
+
+
+def gather_around(x, axis, dim):
+    size = lax.axis_size(axis)
+    pairs = [(i, (i + 1) % size) for i in range(size)]
+    back = [(b, a) for a, b in pairs]
+    lower, upper = ([], [])
+    for step in range(size - 1):
+        if step % 2 == 0:
+            lower.append(lax.ppermute(lower[-1] if lower else x, axis, pairs))
+        else:
+            upper.append(lax.ppermute(upper[-1] if upper else x, axis, back))
+    pieces = jnp.stack([*lower[::-1], x, *upper])
+    shift = lax.axis_index(axis) - len(lower)
+    pieces = pieces[(jnp.arange(size) - shift) % size]
+    return laid_out(pieces, dim)
 
 
 def rotary_embedding(vectors, token_positions):
@@ -49,7 +71,7 @@
     dealt = jnp.einsum("rm,mtd->rtd", chooser, piece, preferred_element_type=jnp.float32).astype(
         jnp.bfloat16
     )
-    widened = lax.all_gather(dealt, "tp", axis=2, tiled=True).astype(jnp.float32)
+    widened = gather_around(dealt, "tp", 2).astype(jnp.float32)
     normalized_input = (
         widened
         * lax.rsqrt(jnp.mean(widened * widened, axis=-1, keepdims=True) + NORM_EPSILON)

time: 285 us -> 333 us (1.17)
  local copies, waits for them, and re-layouts: 8.1 us -> 48.4 us
  starting transfers between devices: 0.12 us -> 9.28 us
  waiting for transfers between devices: 205 us -> 197 us
  other arithmetic: 17 us -> 21.5 us
    all_gather x1 -> x0, waiting for transfers between devices: 19 us -> none  [body(): lax.all_gather(dealt, 'tp', axis=2, tiled=True).astype(jnp.float32)]
    ppermute x0 -> x7, waiting for transfers between devices: none -> 18.7 us  [the longest x4 11.4 us: gather_around(): lower.append(lax.ppermute(lower[-1] if lower else x, axis, pairs))]
    convert_element_type x0 -> x3, local copies, waits for them, and re-layouts: none -> 18.4 us  [the longest x2 13.5 us: body(): widened = gather_around(dealt, 'tp', 2).astype(jnp.float32)]
    unnamed x19 -> x36, local copies, waits for them, and re-layouts: 4.52 us -> 18.7 us
    ppermute x0 -> x7, starting transfers between devices: none -> 9.21 us  [the longest x3 9.2 us: gather_around(): upper.append(lax.ppermute(upper[-1] if upper else x, axis, back))]
    gather x0 -> x1, local copies, waits for them, and re-layouts: none -> 4.59 us  [gather_around(): pieces = pieces[(jnp.arange(size) - shift) % size]]
    psum x1, waiting for transfers between devices: 78.8 us -> 74.6 us  [body(): summed = lax.psum(partials, 'tp')]
  transfers between devices with their start and end apart: 3 -> 9, of which waited for: 3 -> 8; matrix products, arithmetic and copies ran while one was open for 4% -> 6% of each run, Pallas kernels for 0% -> 0%
where the time goes in v1:
time: 333 us
  waiting for transfers between devices  197 us (59%)
  local copies, waits for them, and re-layouts  48.4 us (15%)
  matrix products  42 us (13%)
  other arithmetic  21.5 us (6%)
  between operations  14.5 us (4%)
  starting transfers between devices  9.28 us (3%)
    all_gather x1, waiting for transfers between devices, body(): piece = lax.all_gather(hidden_in, 'req', axis=0, tiled=True)  103 us
    psum x1, waiting for transfers between devices, body(): summed = lax.psum(partials, 'tp')  74.6 us
    unnamed x36, local copies, waits for them, and re-layouts  18.7 us
    convert_element_type x2, local copies, waits for them, and re-layouts, body(): widened = gather_around(dealt, 'tp', 2).astype(jnp.float32)  13.5 us
    dot_general x1, matrix products, body(): jnp.einsum('rm,mtd->rtd', chooser, piece, preferred_element_type=jnp.floa...  11.9 us
    ppermute x4, waiting for transfers between devices, gather_around(): lower.append(lax.ppermute(lower[-1] if lower else x, axis, pairs))  11.4 us
    dot_general x1, matrix products, body(): jnp.einsum('rgqtc,rgcd->rtgqd', cache_weights, cached_values, preferred_e...  10.5 us
    reduce_sum x2, other arithmetic, body(): row_total = jnp.sum(cache_exp, axis=-1) + jnp.sum(tree_exp, axis=-1)  9.38 us
  transfers between devices with their start and end apart: 9, of which 8 were waited for; matrix products, arithmetic and copies ran while one was open for 6% of the time, Pallas kernels for 0%

profile of v1, /device:TPU:2, one launch (start us, length us, event | category | flops | bytes accessed | tf_op | source)
XLA Modules:
  0.0 332.6 jit_solution(4142107959869707690)
XLA Ops:
  7.2 0.7 all-gather.2.cloned.1.call-update
  8.0 1.3 gather_fusion
  9.3 1.2 convolution_minimum_fusion.6
  11.9 0.7 iota_compare_fusion.1
  12.6 102.8 %all-gather.2.cloned.1.call-done = bf16[192,64,384]{2,1,0:T(8,128)(2,1)} async-done(((bf16[6,64,384]{2,1,0:T(8,128)(2,1)}), bf16[192,64,384]{2,1,0:T(8,128)(2,1)}) %all-gather.2.cloned.1.call-update) | async-done | bytes 9437200 | tf_op jit(solution)/shard_map/all_gather | solution.py:68
  115.4 11.9 %fusion.29 = bf16[6,64,384]{2,0,1:T(8,128)(2,1)S(1)} fusion(bf16[192,64,384]{2,1,0:T(8,128)(2,1)} %all-gather.2.cloned.1.call-done, s32[6]{0:T(128)S(1)} %gather_fusion), kind=kOutput, calls=%fused_computation.37 | convolution fusion | flops 56771712 | bytes 9732120 | tf_op jit(solution)/shard_map/rm,mtd->rtd/dot_general | solution.py:71
  127.7 0.4 fusion.78
  128.2 7.7 %collective-permute-done = bf16[6,64,384]{2,0,1:T(8,128)(2,1)} collective-permute-done((bf16[6,64,384]{2,0,1:T(8,128)(2,1)S(1)}, bf16[6,64,384]{2,0,1:T(8,128)(2,1)}, u32[]{:S(2)}, u32[]{:S(2)}) %collective-permute-start) | collective-permute-done | bytes 294944 | tf_op jit(solution)/shard_map/ppermute | solution.py:23
  136.1 4.5 %copy.55 = bf16[3072,384]{0,1:T(8,128)(2,1)} copy(bf16[3072,384]{1,0:T(8,128)(2,1)} %param.15) | data formatting | bytes 4718592 | tf_op args[3]
  140.5 3.0 collective-permute-start.4
  143.5 1.1 collective-permute-done.1
  144.7 4.1 %collective-permute-done.4 = bf16[6,64,384]{2,0,1:T(8,128)(2,1)S(1)} collective-permute-done((bf16[6,64,384]{2,0,1:T(8,128)(2,1)S(1)}, bf16[6,64,384]{2,0,1:T(8,128)(2,1)S(1)}, u32[]{:S(2)}, u32[]{:S(2)}) %collective-permute-start.4) | collective-permute-done | bytes 294944 | tf_op jit(solution)/shard_map/ppermute | solution.py:25
  148.8 3.1 collective-permute-start.5
  151.9 1.3 collective-permute-done.2
  153.2 0.8 multiply_cosine_fusion.1
  154.0 3.2 collective-permute-done.5
  157.2 3.1 collective-permute-start.6
  160.3 1.3 collective-permute-done.3
  161.6 0.8 bitcast_dynamic-update-slice_fusion.7
  162.4 0.8 bitcast_dynamic-update-slice_fusion.6
  163.2 1.8 bitcast_dynamic-update-slice_fusion.5
  165.0 1.8 bitcast_dynamic-update-slice_fusion.4
  166.8 0.8 bitcast_dynamic-update-slice_fusion.3
  167.6 0.8 bitcast_dynamic-update-slice_fusion.2
  168.4 0.8 bitcast_dynamic-update-slice_fusion.1
  169.1 0.8 bitcast_dynamic-update-slice_fusion
  170.0 4.6 %gather_fusion.1 = bf16[8,6,64,384]{3,1,2,0:T(8,128)(2,1)} fusion(bf16[8,6,64,384]{3,1,2,0:T(8,128)(2,1)} %bitcast_dynamic-update-slice_fusion, s32[1024]{0:T(1024)S(1)} %pad_clamp_fusion), kind=kCustom, calls=%fused_computation.1 | custom fusion | bytes 4718624 | tf_op jit(solution)/shard_map/gather | solution.py:28
  174.5 2.8 fusion.8
  177.6 5.1 %convert_bitcast_fusion = f32[6,64,8,384]{3,0,1,2:T(8,128)} fusion(bf16[8,6,64,384]{3,1,2,0:T(8,128)(2,1)} %gather_fusion.1), kind=kLoop, calls=%fused_computation.8 | loop fusion | flops 1179648 | bytes 7077888 | tf_op jit(solution)/shard_map/convert_element_type | solution.py:74
  182.7 1.0 fusion.14
  183.8 2.9 copy.54
  186.6 4.9 %reshape.362 = bf16[6,64,3072,1]{2,1,0,3:T(8,128)(2,1)} reshape(bf16[6,64,8,384]{3,2,1,0:T(8,128)(2,1)} %copy.54) | data formatting | bytes 4718592 | tf_op jit(solution)/shard_map/convert_element_type | solution.py:79
  191.5 7.7 %copy.59 = f32[6,64,8,384]{3,2,1,0:T(8,128)} copy(f32[6,64,8,384]{3,0,1,2:T(8,128)} %convert_bitcast_fusion) | data formatting | bytes 9437184 | tf_op jit(solution)/shard_map/convert_element_type | solution.py:74
  199.3 5.8 %reshape.343 = f32[6,64,3072]{2,1,0:T(8,128)} reshape(f32[6,64,8,384]{3,2,1,0:T(8,128)} %copy.59) | data formatting | bytes 9437184 | tf_op jit(solution)/shard_map/convert_element_type | solution.py:74
  205.1 5.9 %copy.76 = f32[48,8,8,384]{3,1,2,0:T(8,128)} copy(f32[48,8,8,384]{3,2,1,0:T(8,128)} %bitcast.168) | data formatting | bytes 9437184
  210.9 2.1 fusion.35
  213.1 0.8 fusion.51
  213.9 1.4 fusion.17
  215.7 6.9 %fusion.2 = (f32[6,3,64]{2,1,0:T(4,128)S(1)}, f32[6,64,3,3456]{3,1,2,0:T(8,128)}) fusion(pred[6,3456]{1,0:T(8,128)(4,1)S(1)} %iota_compare_fusion.1, bf16[6,1,3456,128]{3,2,1,0:T(8,128)(2,1)S(1)} %bitcast.173, bf16[6,64,3,64]{3,1,2,0:T(8,128)(2,1)S(1)} %get-tuple-element.11, bf16[6,64,3,64]{3,1,2,0:T(8,128)(2,1)S(1)} %get-tuple-element.10), kind=kOutput, calls=%fused_computation.7 | convolution fusion | flops 1031748480 | bytes 21553920 | tf_op jit(solution)/shard_map/rtgqd,rgcd->rgqtc/dot_general | solution.py:110
  222.5 0.4 fusion.79
  223.1 9.2 %fusion.1 = f32[6,3,64]{2,1,0:T(4,128)S(1)} fusion(f32[6,64,3,3456]{3,1,2,0:T(8,128)} %get-tuple-element.19, f32[6,3,64]{2,1,0:T(4,128)S(1)} %max.9, pred[6,3456]{1,0:T(8,128)(4,1)S(1)} %iota_compare_fusion.1), kind=kLoop, calls=%fused_computation.6 | loop fusion | flops 15924096 | bytes 15955200 | tf_op jit(solution)/shard_map/reduce_sum | solution.py:125
  232.4 10.5 %fusion.24 = f32[6,128,3,64]{1,3,2,0:T(8,128)S(1)} fusion(bf16[6,1,3456,128]{3,2,1,0:T(8,128)(2,1)} %param.20, f32[6,3,64]{2,1,0:T(4,128)S(1)} %add.126, f32[6,3,64]{2,1,0:T(4,128)S(1)} %max.9, f32[6,64,3,3456]{3,1,2,0:T(8,128)} %get-tuple-element.19, pred[6,3456]{1,0:T(8,128)(4,1)S(1)} %iota_compare_fusion.1), kind=kOutput, calls=%fused_computation.36 | convolution fusion | flops 1039122432 | bytes 21853440 | tf_op jit(solution)/shard_map/rgqtc,rgcd->rtgqd/dot_general | solution.py:128
  243.0 0.8 fusion.36
  244.4 3.6 %fusion.41 = f32[384,3072]{1,0:T(8,128)} fusion(bf16[384,3072]{1,0:T(8,128)(2,1)S(1)} %copy-done, bf16[48,8,3,128]{3,2,1,0:T(4,128)(2,1)S(1)} %bitcast.176), kind=kOutput, calls=%fused_computation.68 | convolution fusion | flops 905969664 | bytes 7372800 | tf_op jit(solution)/shard_map/dot_general | solution.py:142
  248.0 0.8 fusion.37
  248.9 74.6 %all-reduce.2.cloned.1.call-done = f32[384,3072]{1,0:T(8,128)} async-done(((f32[384,3072]{1,0:T(8,128)}), f32[384,3072]{1,0:T(8,128)}) %all-reduce.2.cloned.1.call-update) | async-done | bytes 4718608 | tf_op jit(solution)/shard_map/psum | solution.py:145
  323.5 1.1 constant_dynamic-slice_fusion
  325.0 0.8 copy.65
  (65 shorter events, 3.7 us)
Async XLA Ops:
  7.2 237.2 %copy-start = (bf16[384,3072]{1,0:T(8,128)(2,1)S(1)}, bf16[384,3072]{1,0:T(8,128)(2,1)}, u32[]{:S(2)}) copy-start(bf16[384,3072]{1,0:T(8,128)(2,1)} %param.18) | copy-start | bytes 7077892
  7.2 108.2 %all-gather.2.cloned.1.call-start = ((), (), s32[]{:S(2)}) async-start(), calls=%async_computation | async-start | bytes 9732096 | tf_op jit(solution)/shard_map/all_gather | solution.py:68
  7.9 315.6 %all-reduce.2.cloned.1.call-start = ((), (), s32[]{:S(2)}) async-start(), calls=%async_computation.1 | async-start | bytes 9437184 | tf_op jit(solution)/shard_map/psum | solution.py:145
  12.6 115.1 %copy-start.7 = (s32[6]{0:T(128)S(1)}, s32[6]{0:T(128)}, u32[]{:S(2)}) copy-start(s32[6]{0:T(128)} %param.21) | copy-start | bytes 76
  12.6 115.1 %copy-start.6 = (bf16[3072]{0:T(1024)(128)(2,1)S(1)}, bf16[3072]{0:T(1024)(128)(2,1)}, u32[]{:S(2)}) copy-start(bf16[3072]{0:T(1024)(128)(2,1)} %param.14) | copy-start | bytes 18436
  127.3 8.5 %collective-permute-start = (bf16[6,64,384]{2,0,1:T(8,128)(2,1)S(1)}, bf16[6,64,384]{2,0,1:T(8,128)(2,1)}, u32[]{:S(2)}, u32[]{:S(2)}) collective-permute-start(bf16[6,64,384]{2,0,1:T(8,128)(2,1)S(1)} %fusion.29), channel_id=1, source_target_pairs={{0,1},{1,2},{2,3},{3,4},{4,5},{5,6},{6,7},{7,0},{8,9},{9,10},{10,1... | collective-permute-start | bytes 884744 | tf_op jit(solution)/shard_map/ppermute | solution.py:23
  135.9 8.7 %collective-permute-start.1 = (bf16[6,64,384]{2,0,1:T(8,128)(2,1)}, bf16[6,64,384]{2,0,1:T(8,128)(2,1)}, u32[]{:S(2)}, u32[]{:S(2)}) collective-permute-start(bf16[6,64,384]{2,0,1:T(8,128)(2,1)} %collective-permute-done), channel_id=1, source_target_pairs={{0,1},{1,2},{2,3},{3,4},{4,5},{5,6},{6,7},{7,0},{8,9},{9,10},{10,1... | collective-permute-start | bytes 884744 | tf_op jit(solution)/shard_map/ppermute | solution.py:23
  140.5 8.3 %collective-permute-start.4 = (bf16[6,64,384]{2,0,1:T(8,128)(2,1)S(1)}, bf16[6,64,384]{2,0,1:T(8,128)(2,1)S(1)}, u32[]{:S(2)}, u32[]{:S(2)}) collective-permute-start(bf16[6,64,384]{2,0,1:T(8,128)(2,1)S(1)} %fusion.29), channel_id=1, source_target_pairs={{1,0},{2,1},{3,2},{4,3},{5,4},{6,5},{7,6},{0,7},{9,8},{10,9},{11,1... | collective-permute-start | bytes 884744 | tf_op jit(solution)/shard_map/ppermute | solution.py:25
  144.6 8.6 %collective-permute-start.2 = (bf16[6,64,384]{2,0,1:T(8,128)(2,1)}, bf16[6,64,384]{2,0,1:T(8,128)(2,1)S(1)}, u32[]{:S(2)}, u32[]{:S(2)}) collective-permute-start(bf16[6,64,384]{2,0,1:T(8,128)(2,1)} %collective-permute-done.1), channel_id=1, source_target_pairs={{0,1},{1,2},{2,3},{3,4},{4,5},{5,6},{6,7},{7,0},{8,9},{9,10},{10,1... | collective-permute-start | bytes 884744 | tf_op jit(solution)/shard_map/ppermute | solution.py:23
  148.8 8.4 %collective-permute-start.5 = (bf16[6,64,384]{2,0,1:T(8,128)(2,1)S(1)}, bf16[6,64,384]{2,0,1:T(8,128)(2,1)S(1)}, u32[]{:S(2)}, u32[]{:S(2)}) collective-permute-start(bf16[6,64,384]{2,0,1:T(8,128)(2,1)S(1)} %collective-permute-done.4), channel_id=1, source_target_pairs={{1,0},{2,1},{3,2},{4,3},{5,4},{6,5},{7,6},{0,7},{9,8},{10,9},{11,1... | collective-permute-start | bytes 884744 | tf_op jit(solution)/shard_map/ppermute | solution.py:25
  153.2 8.4 %collective-permute-start.3 = (bf16[6,64,384]{2,0,1:T(8,128)(2,1)S(1)}, bf16[6,64,384]{2,0,1:T(8,128)(2,1)S(1)}, u32[]{:S(2)}, u32[]{:S(2)}) collective-permute-start(bf16[6,64,384]{2,0,1:T(8,128)(2,1)S(1)} %collective-permute-done.2), channel_id=1, source_target_pairs={{0,1},{1,2},{2,3},{3,4},{4,5},{5,6},{6,7},{7,0},{8,9},{9,10},{10,1... | collective-permute-start | bytes 884744 | tf_op jit(solution)/shard_map/ppermute | solution.py:23
  157.2 11.9 %collective-permute-start.6 = (bf16[6,64,384]{2,0,1:T(8,128)(2,1)S(1)}, bf16[6,64,384]{2,0,1:T(8,128)(2,1)S(1)}, u32[]{:S(2)}, u32[]{:S(2)}) collective-permute-start(bf16[6,64,384]{2,0,1:T(8,128)(2,1)S(1)} %collective-permute-done.5), channel_id=1, source_target_pairs={{1,0},{2,1},{3,2},{4,3},{5,4},{6,5},{7,6},{0,7},{9,8},{10,9},{11,1... | collective-permute-start | bytes 884744 | tf_op jit(solution)/shard_map/ppermute | solution.py:25
  177.6 5.1 %copy-start.1 = (bf16[8,6,64,384]{3,1,2,0:T(8,128)(2,1)S(1)}, bf16[8,6,64,384]{3,1,2,0:T(8,128)(2,1)}, u32[]{:S(2)}) copy-start(bf16[8,6,64,384]{3,1,2,0:T(8,128)(2,1)} %gather_fusion.1) | copy-start | bytes 7077892
  205.1 5.9 %copy-start.2 = (f32[6,64,3072]{2,1,0:T(8,128)S(1)}, f32[6,64,3072]{2,1,0:T(8,128)}, u32[]{:S(2)}) copy-start(f32[6,64,3072]{2,1,0:T(8,128)} %reshape.343) | copy-start | bytes 14155780
  205.1 8.8 %copy-start.3 = (bf16[3072,384]{0,1:T(8,128)(2,1)S(1)}, bf16[3072,384]{0,1:T(8,128)(2,1)}, u32[]{:S(2)}) copy-start(bf16[3072,384]{0,1:T(8,128)(2,1)} %copy.55) | copy-start | bytes 7077892
  205.1 8.8 %copy-start.4 = (bf16[6,64,3072,1]{2,1,0,3:T(8,128)(2,1)S(1)}, bf16[6,64,3072,1]{2,1,0,3:T(8,128)(2,1)}, u32[]{:S(2)}) copy-start(bf16[6,64,3072,1]{2,1,0,3:T(8,128)(2,1)} %reshape.362) | copy-start | bytes 7077892
  210.9 4.7 %slice-start.2 = ((s8[5308416]{0:T(1024)(128)(4,1)}), s8[4194304]{0:T(1024)(128)(4,1)S(1)}, s32[]{:S(2)}) async-start(s8[5308416]{0:T(1024)(128)(4,1)} %bitcast.172), calls=%async_computation.4 | async-start | bytes 8388608
  213.9 1.7 slice-start.3
  223.1 19.8 %slice-start = ((s8[4718592]{0:T(1024)(128)(4,1)}), s8[524288]{0:T(1024)(128)(4,1)S(1)}, s32[]{:S(2)}) async-start(s8[4718592]{0:T(1024)(128)(4,1)} %bitcast.169), calls=%async_computation.2 | async-start | bytes 1048576
  232.4 10.5 %slice-start.1 = ((s8[4718592]{0:T(1024)(128)(4,1)}), s8[4194304]{0:T(1024)(128)(4,1)S(1)}, s32[]{:S(2)}) async-start(s8[4718592]{0:T(1024)(128)(4,1)} %bitcast.169), calls=%async_computation.3 | async-start | bytes 8388608
  232.4 10.5 %copy-start.5 = (bf16[3072,128]{1,0:T(8,128)(2,1)S(1)}, bf16[3072,128]{1,0:T(8,128)(2,1)}, u32[]{:S(2)}) copy-start(bf16[3072,128]{1,0:T(8,128)(2,1)} %param.17) | copy-start | bytes 2359300
  244.4 3.6 %copy-start.8 = (s32[6,8]{1,0:T(8,128)S(1)}, s32[6,8]{1,0:T(8,128)}, u32[]{:S(2)}) copy-start(s32[6,8]{1,0:T(8,128)} %param.23) | copy-start | bytes 580
Sparse Core Ops, SparseCore 0:
  10.6 104.8 all-gather.1
  248.1 75.3 all-reduce.1
